TPU v7x, 512 devices: a whole 4x4x16 slice. The times are simulated.
512 devices in a mesh: segment: 2 (over x_hi), tile: 32 (over x_lo, z), stream: 8 (over y, core).
Axes of the slice: x: 4 (x_hi: 2, x_lo: 2; x = x_hi * 2 + x_lo), y: 4, z: 16, core: 2. Of those that a mesh axis runs over, the one named last changes fastest.
Arguments:
- frames: bfloat16 [8, 16, 2048, 256], P(None, 'stream', 'tile'), parts along dimension 1, may hold values from -6 to 6
- spatial_weight: bfloat16 [2, 2, 2304, 256], P('segment'), may hold values from -0.125 to 0.125
- temporal_weight: bfloat16 [2, 2, 768, 256], P('segment'), may hold values from -0.21875 to 0.21875
- ramp: int32 [32, 96], P('tile'), may hold values from 1 to 16
- intersection: int32 [32, 2], P('tile'), may hold values from 1 to 16, as said below
Outputs:
- encoded: bfloat16 [8, 16, 2048, 256], P('segment', 'stream', 'tile'), parts along dimension 1
There are 8 independent parts, one for each index of `stream`. A program takes and returns all parts, laid end to end along the dimension named above; an argument that names none is the same for every part. Nothing has to cross between parts.
Inputs may be any that keep to these rules, and one draw needn't show every extreme that they name: `intersection`: each tile's two widths lie in 1 to 16; some tile has both equal to 16.
All inputs are finite; a program needn't handle non-finite values.
Results may differ from a plain program's by a relative error of at most 0.014.
Values may be sent and summed in bfloat16 or wider, within the bound.
A program may use at most 64 MiB of HBM per device.

v0:
```python
import jax
import jax.numpy as jnp
from jax import lax
from jax.sharding import PartitionSpec as P

GROUPS = 32
MARGIN = 16


def passed_along(value, axis, steps):
    count = lax.axis_size(axis)
    leading, last = (max(0, -steps), min(count, count - steps))
    return lax.ppermute(value, axis, [(source, source + steps) for source in range(leading, last)])


def padded_2(cells, sides, width):
    for axis, dim in sides:
        count = lax.axis_size(axis)
        ends = count - 1
        head = lax.slice_in_dim(cells, 0, width, axis=dim)
        tail = lax.slice_in_dim(cells, cells.shape[dim] - width, cells.shape[dim], axis=dim)
        cells = jnp.concatenate(
            [
                lax.ppermute(tail, axis, [(i, (i + 1) % count) for i in range(ends)]),
                cells,
                lax.ppermute(head, axis, [((i + 1) % count, i) for i in range(ends)]),
            ],
            axis=dim,
        )
    return cells


def norm_silu(hidden):
    channels = hidden.shape[-1]
    group_width = channels // GROUPS
    chan_mean = jnp.mean(hidden, axis=(1, 2))
    group_mean = jnp.repeat(
        jnp.mean(chan_mean.reshape(-1, GROUPS, group_width), axis=2), group_width, axis=1
    )
    centered = hidden - group_mean[:, None, None, :]
    chan_var = jnp.mean(centered * centered, axis=(1, 2))
    group_var = jnp.repeat(
        jnp.mean(chan_var.reshape(-1, GROUPS, group_width), axis=2), group_width, axis=1
    )
    return jax.nn.silu(centered * lax.rsqrt(group_var + 1e-06)[:, None, None, :])


def spatial_conv(activity, weight):
    frame_count, row_count, column_count, channels = activity.shape
    padded = jnp.pad(activity, ((0, 0), (1, 1), (1, 1), (0, 0)))
    pieces = [
        padded[:, shift_row : shift_row + row_count, shift_col : shift_col + column_count, :]
        for shift_row in range(3)
        for shift_col in range(3)
    ]
    stacked = jnp.concatenate(pieces, axis=-1).reshape(-1, 9 * channels)
    product = jnp.dot(stacked, weight, preferred_element_type=jnp.float32)
    return product.reshape(frame_count, row_count, column_count, -1)


def temporal_conv(spatial_out, weight, prior):
    frame_count = spatial_out.shape[0]
    sequence = jnp.concatenate([prior, spatial_out], axis=0)
    stacked = jnp.concatenate(
        [sequence[0:frame_count], sequence[1 : frame_count + 1], sequence[2 : frame_count + 2]],
        axis=-1,
    )
    product = jnp.dot(
        stacked.reshape(-1, stacked.shape[-1]), weight, preferred_element_type=jnp.float32
    )
    return (product.reshape(spatial_out.shape), sequence[frame_count:])


def residual_block(block_in, spatial_weights, temporal_weights, priors):
    hidden = block_in.astype(jnp.float32)
    new_priors = []
    for conv_index in range(2):
        activity = norm_silu(hidden).astype(jnp.bfloat16)
        spatial_out = spatial_conv(activity, spatial_weights[conv_index]).astype(jnp.bfloat16)
        hidden, state = temporal_conv(spatial_out, temporal_weights[conv_index], priors[conv_index])
        new_priors.append(state)
    result = (block_in.astype(jnp.float32) + hidden).astype(jnp.bfloat16)
    return (result, jnp.stack(new_priors))


def margin_weights(ramp, intersection, window_width):
    positions = jnp.arange(window_width)
    inside = (positions >= MARGIN - intersection[0, 0]) & (
        positions < window_width - MARGIN + intersection[0, 1]
    )
    return jnp.where(inside, ramp[0].astype(jnp.float32), 0.0)


def blend_columns(latents, weights_vec):
    owned = latents.shape[2] - 2 * MARGIN
    weights_wire = weights_vec.astype(jnp.bfloat16)
    right_lat, right_weight = passed_along(
        (latents[:, :, :MARGIN, :], weights_wire[:MARGIN]), "tile", -1
    )
    left_lat, left_weight = passed_along(
        (latents[:, :, MARGIN + owned :, :], weights_wire[MARGIN + owned :]), "tile", 1
    )
    own_weight = weights_vec[MARGIN : MARGIN + owned]
    numer = (
        latents[:, :, MARGIN : MARGIN + owned, :].astype(jnp.float32)
        * own_weight[None, None, :, None]
    )
    denom = own_weight
    left_factor = left_weight.astype(jnp.float32)
    left_term = left_lat.astype(jnp.float32) * left_factor[None, None, :, None]
    numer = numer + jnp.pad(left_term, ((0, 0), (0, 0), (0, owned - MARGIN), (0, 0)))
    denom = denom + jnp.pad(left_factor, (0, owned - MARGIN))
    right_factor = right_weight.astype(jnp.float32)
    right_term = right_lat.astype(jnp.float32) * right_factor[None, None, :, None]
    numer = numer + jnp.pad(right_term, ((0, 0), (0, 0), (owned - MARGIN, 0), (0, 0)))
    denom = denom + jnp.pad(right_factor, (owned - MARGIN, 0))
    return (numer / denom[None, None, :, None]).astype(jnp.bfloat16)


def body(frames, spatial_weight, temporal_weight, ramp, intersection):
    segment = lax.axis_index("segment")
    extended = padded_2(frames, (("tile", 2),), MARGIN)
    weights_vec = margin_weights(ramp, intersection, extended.shape[2])
    frame_total = frames.shape[0]
    half_count = frame_total // 2
    group_count = 2
    group_size = frame_total // group_count
    received = jnp.zeros((group_size,) + extended.shape[1:], jnp.bfloat16)
    priors = jnp.zeros((2, 2) + extended.shape[1:], jnp.bfloat16)
    finished = []
    for tick_index in range(group_count + 1):
        if tick_index < group_count:
            fresh_input = extended[tick_index * group_size : (tick_index + 1) * group_size]
        else:
            fresh_input = jnp.zeros_like(received)
        block_in = jnp.where(segment == 0, fresh_input, received)
        block_out, new_priors = residual_block(
            block_in, spatial_weight[0], temporal_weight[0], priors
        )
        active = (tick_index - segment >= 0) & (tick_index - segment < group_count)
        priors = jnp.where(active, new_priors, priors)
        if tick_index > 0:
            finished.append(block_out)
        if tick_index < group_count:
            received = passed_along(block_out, "segment", 1)
    latents = jnp.concatenate(finished, axis=0)
    blended = blend_columns(latents, weights_vec)
    returned = passed_along(blended[:half_count], "segment", -1)
    result = jnp.where(segment == 0, returned, blended[half_count:])
    return result


def solution(mesh):
    in_specs = (
        P(None, "stream", "tile", None),
        P("segment", None, None, None),
        P("segment", None, None, None),
        P("tile", None),
        P("tile", None),
    )
    out_specs = P("segment", "stream", "tile", None)
    return jax.shard_map(body, mesh=mesh, in_specs=in_specs, out_specs=out_specs, check_vma=False)
```

profile of v0, /device:TPU:26, one launch (start us, length us, event | category | flops | bytes accessed | tf_op | source)
XLA Modules:
  0.0 98.7 jit_solution(6341125337387812358)
XLA Ops:
  0.0 1.0 %fusion.152 = (bf16[8,2,16,256]{3,2,1,0:T(8,128)(2,1)S(1)}, bf16[8,2,16,256]{3,2,1,0:T(8,128)(2,1)S(1)}) fusion(bf16[8,2,64,256]{3,2,1,0:T(8,128)(2,1)} %param.5), kind=kLoop, calls=%fused_computation.290 | loop fusion | bytes 524288 | tf_op jit(solution)/shard_map/slice | solution.py:20
  1.0 3.8 %collective-permute-start = (bf16[8,2,16,256]{3,2,1,0:T(8,128)(2,1)S(1)}, bf16[8,2,16,256]{3,2,1,0:T(8,128)(2,1)S(1)}, u32[]{:S(2)}, u32[]{:S(2)}) collective-permute-start(bf16[8,2,16,256]{3,2,1,0:T(8,128)(2,1)S(1)} %get-tuple-element.12), channel_id=1, source_target_pairs={{0,8},{8,16},{16,24},{24,32},{32,40},{40,48},{48,56},{56,64},{64,7... | collective-permute-start | bytes 393224 | tf_op jit(solution)/shard_map/ppermute | solution.py:24
  4.8 1.4 %fusion.155 = (s32[1,1]{1,0:T(1,128)}, s32[1,1]{1,0:T(1,128)}) fusion(s32[1,2]{1,0:T(1,128)} %param.9), kind=kLoop, calls=%fused_computation.293 | loop fusion | bytes 16 | tf_op jit(solution)/shard_map/slice | solution.py:88
  7.6 0.7 fusion.151
  8.3 3.8 %collective-permute-start.5 = (bf16[16]{0:T(256)(128)(2,1)S(1)}, bf16[16]{0:T(256)(128)(2,1)S(1)}, u32[]{:S(2)}, u32[]{:S(2)}) collective-permute-start(bf16[16]{0:T(256)(128)(2,1)S(1)} %get-tuple-element.23), channel_id=1, source_target_pairs={{0,8},{8,16},{16,24},{24,32},{32,40},{40,48},{48,56},{56,64},{64,7... | collective-permute-start | bytes 104 | tf_op jit(solution)/shard_map/ppermute | solution.py:13
  12.1 7.6 %collective-permute-start.7 = (bf16[16]{0:T(256)(128)(2,1)S(1)}, bf16[16]{0:T(256)(128)(2,1)S(1)}, u32[]{:S(2)}, u32[]{:S(2)}) collective-permute-start(bf16[16]{0:T(256)(128)(2,1)S(1)} %get-tuple-element.24), channel_id=1, source_target_pairs={{8,0},{16,8},{24,16},{32,24},{40,32},{48,40},{56,48},{64,56},{72,6... | collective-permute-start | bytes 104 | tf_op jit(solution)/shard_map/ppermute | solution.py:13
  19.7 3.9 %collective-permute-start.1 = (bf16[8,2,16,256]{3,2,1,0:T(8,128)(2,1)S(1)}, bf16[8,2,16,256]{3,2,1,0:T(8,128)(2,1)S(1)}, u32[]{:S(2)}, u32[]{:S(2)}) collective-permute-start(bf16[8,2,16,256]{3,2,1,0:T(8,128)(2,1)S(1)} %get-tuple-element.11), channel_id=1, source_target_pairs={{8,0},{16,8},{24,16},{32,24},{40,32},{48,40},{56,48},{64,56},{72,6... | collective-permute-start | bytes 393224 | tf_op jit(solution)/shard_map/ppermute | solution.py:26
  23.7 1.1 %constant_dynamic-update-slice_fusion.1 = bf16[8,2,96,256]{3,2,1,0:T(8,128)(2,1)S(1)} fusion(bf16[8,2,96,256]{3,2,1,0:T(8,128)(2,1)S(1)} %constant_dynamic-update-slice_fusion.2, bf16[8,2,64,256]{3,2,1,0:T(8,128)(2,1)} %param.5), kind=kLoop, calls=%fused_computation.249 | loop fusion | bytes 1048576
  24.8 1.8 %collective-permute-done.1 = bf16[8,2,16,256]{3,2,1,0:T(8,128)(2,1)S(1)} collective-permute-done((bf16[8,2,16,256]{3,2,1,0:T(8,128)(2,1)S(1)}, bf16[8,2,16,256]{3,2,1,0:T(8,128)(2,1)S(1)}, u32[]{:S(2)}, u32[]{:S(2)}) %collective-permute-start.1) | collective-permute-done | bytes 131104 | tf_op jit(solution)/shard_map/ppermute | solution.py:26
  27.6 0.3 fusion.67
  28.2 0.3 constant_dynamic-update-slice_fusion.3
  28.7 0.9 copy-done
  29.6 1.1 %convolution_convert_fusion.5 = bf16[4,2,96,256]{3,2,1,0:T(8,128)(2,1)S(1)} fusion(bf16[4,2,96,2304]{3,2,1,0:T(8,128)(2,1)S(1)} %fusion.91, bf16[1,2,2304,256]{3,2,1,0:T(8,128)(2,1)S(1)} %copy-done), kind=kOutput, calls=%fused_computation.59 | convolution fusion | flops 906166272 | bytes 5111808 | tf_op jit(solution)/shard_map/dot_general | solution.py:57
  30.7 0.5 fusion.156
  32.1 0.3 multiply_convert_fusion.2
  32.7 0.3 constant_dynamic-update-slice_fusion.4
  33.2 0.9 copy-done.1
  34.1 1.1 %convolution_convert_fusion.4 = bf16[4,2,96,256]{3,2,1,0:T(8,128)(2,1)S(1)} fusion(bf16[4,2,96,2304]{3,2,1,0:T(8,128)(2,1)S(1)} %fusion.99, bf16[1,2,2304,256]{3,2,1,0:T(8,128)(2,1)S(1)} %copy-done.1), kind=kOutput, calls=%fused_computation.58 | convolution fusion | flops 906166272 | bytes 5111808 | tf_op jit(solution)/shard_map/dot_general | solution.py:57
  35.3 0.5 fusion
  35.7 4.3 %collective-permute-start.2 = (bf16[4,2,96,256]{3,2,1,0:T(8,128)(2,1)S(1)}, bf16[4,2,96,256]{3,2,1,0:T(8,128)(2,1)S(1)}, u32[]{:S(2)}, u32[]{:S(2)}) collective-permute-start(bf16[4,2,96,256]{3,2,1,0:T(8,128)(2,1)S(1)} %fusion), channel_id=1, source_target_pairs={{0,256},{1,257},{2,258},{3,259},{4,260},{5,261},{6,262},{7,263},{8... | collective-permute-start | bytes 1179656 | tf_op jit(solution)/shard_map/ppermute | solution.py:13
  40.2 6.8 %collective-permute-done.2 = bf16[4,2,96,256]{3,2,1,0:T(8,128)(2,1)S(1)} collective-permute-done((bf16[4,2,96,256]{3,2,1,0:T(8,128)(2,1)S(1)}, bf16[4,2,96,256]{3,2,1,0:T(8,128)(2,1)S(1)}, u32[]{:S(2)}, u32[]{:S(2)}) %collective-permute-start.2) | collective-permute-done | bytes 393248 | tf_op jit(solution)/shard_map/ppermute | solution.py:13
  49.1 0.9 copy-done.2
  50.0 1.1 %convolution_convert_fusion.3 = bf16[4,2,96,256]{3,2,1,0:T(8,128)(2,1)S(1)} fusion(bf16[4,2,96,2304]{3,2,1,0:T(8,128)(2,1)S(1)} %fusion.107, bf16[1,2,2304,256]{3,2,1,0:T(8,128)(2,1)S(1)} %copy-done.2), kind=kOutput, calls=%fused_computation.57 | convolution fusion | flops 906166272 | bytes 5111808 | tf_op jit(solution)/shard_map/dot_general | solution.py:57
  51.1 0.5 fusion.157
  52.5 0.3 multiply_convert_fusion.1
  53.1 0.3 constant_dynamic-update-slice_fusion.6
  53.6 0.9 copy-done.3
  54.6 1.1 %convolution_convert_fusion.2 = bf16[4,2,96,256]{3,2,1,0:T(8,128)(2,1)S(1)} fusion(bf16[4,2,96,2304]{3,2,1,0:T(8,128)(2,1)S(1)} %fusion.115, bf16[1,2,2304,256]{3,2,1,0:T(8,128)(2,1)S(1)} %copy-done.3), kind=kOutput, calls=%fused_computation.56 | convolution fusion | flops 906166272 | bytes 5111808 | tf_op jit(solution)/shard_map/dot_general | solution.py:57
  55.7 0.5 fusion.1
  56.2 6.1 %collective-permute-start.3 = (bf16[4,2,96,256]{3,2,1,0:T(8,128)(2,1)S(1)}, bf16[4,2,96,256]{3,2,1,0:T(8,128)(2,1)S(1)}, u32[]{:S(2)}, u32[]{:S(2)}) collective-permute-start(bf16[4,2,96,256]{3,2,1,0:T(8,128)(2,1)S(1)} %fusion.1), channel_id=1, source_target_pairs={{0,256},{1,257},{2,258},{3,259},{4,260},{5,261},{6,262},{7,263},{8... | collective-permute-start | bytes 1179656 | tf_op jit(solution)/shard_map/ppermute | solution.py:13
  62.4 5.7 %collective-permute-done.3 = bf16[4,2,96,256]{3,2,1,0:T(8,128)(2,1)S(1)} collective-permute-done((bf16[4,2,96,256]{3,2,1,0:T(8,128)(2,1)S(1)}, bf16[4,2,96,256]{3,2,1,0:T(8,128)(2,1)S(1)}, u32[]{:S(2)}, u32[]{:S(2)}) %collective-permute-start.3) | collective-permute-done | bytes 393248 | tf_op jit(solution)/shard_map/ppermute | solution.py:13
  69.1 0.3 fusion.75
  69.7 0.3 constant_dynamic-update-slice_fusion.7
  70.2 0.9 copy-done.4
  71.1 1.1 %convolution_convert_fusion.1 = bf16[4,2,96,256]{3,2,1,0:T(8,128)(2,1)S(1)} fusion(bf16[4,2,96,2304]{3,2,1,0:T(8,128)(2,1)S(1)} %fusion.123, bf16[1,2,2304,256]{3,2,1,0:T(8,128)(2,1)S(1)} %copy-done.4), kind=kOutput, calls=%fused_computation.55 | convolution fusion | flops 906166272 | bytes 5111808 | tf_op jit(solution)/shard_map/dot_general | solution.py:57
  72.2 0.5 fusion.158
  73.6 0.3 multiply_convert_fusion
  74.1 0.3 constant_dynamic-update-slice_fusion.8
  74.7 0.9 copy-done.5
  75.6 1.1 %convolution_convert_fusion = bf16[4,2,96,256]{3,2,1,0:T(8,128)(2,1)S(1)} fusion(bf16[4,2,96,2304]{3,2,1,0:T(8,128)(2,1)S(1)} %fusion.131, bf16[1,2,2304,256]{3,2,1,0:T(8,128)(2,1)S(1)} %copy-done.5), kind=kOutput, calls=%fused_computation.54 | convolution fusion | flops 906166272 | bytes 5111808 | tf_op jit(solution)/shard_map/dot_general | solution.py:57
  76.7 0.5 fusion.2
  77.3 2.1 %collective-permute-start.4 = (bf16[8,2,16,256]{3,2,1,0:T(8,128)(2,1)S(1)}, bf16[8,2,16,256]{3,2,1,0:T(8,128)(2,1)S(1)}, u32[]{:S(2)}, u32[]{:S(2)}) collective-permute-start(bf16[8,2,16,256]{3,2,1,0:T(8,128)(2,1)S(1)} %get-tuple-element.9), channel_id=1, source_target_pairs={{0,8},{8,16},{16,24},{24,32},{32,40},{40,48},{48,56},{56,64},{64,7... | collective-permute-start | bytes 393224 | tf_op jit(solution)/shard_map/ppermute | solution.py:13
  79.4 5.9 %collective-permute-start.6 = (bf16[8,2,16,256]{3,2,1,0:T(8,128)(2,1)S(1)}, bf16[8,2,16,256]{3,2,1,0:T(8,128)(2,1)S(1)}, u32[]{:S(2)}, u32[]{:S(2)}) collective-permute-start(bf16[8,2,16,256]{3,2,1,0:T(8,128)(2,1)S(1)} %get-tuple-element.10), channel_id=1, source_target_pairs={{8,0},{16,8},{24,16},{32,24},{40,32},{48,40},{56,48},{64,56},{72,6... | collective-permute-start | bytes 393224 | tf_op jit(solution)/shard_map/ppermute | solution.py:13
  85.3 0.9 collective-permute-done.4
  86.4 1.5 %collective-permute-done.6 = bf16[8,2,16,256]{3,2,1,0:T(8,128)(2,1)S(1)} collective-permute-done((bf16[8,2,16,256]{3,2,1,0:T(8,128)(2,1)S(1)}, bf16[8,2,16,256]{3,2,1,0:T(8,128)(2,1)S(1)}, u32[]{:S(2)}, u32[]{:S(2)}) %collective-permute-start.6) | collective-permute-done | bytes 131104 | tf_op jit(solution)/shard_map/ppermute | solution.py:13
  88.2 1.3 %collective-permute-start.8 = (bf16[4,2,64,256]{3,2,1,0:T(8,128)(2,1)S(1)}, bf16[4,2,64,256]{3,2,1,0:T(8,128)(2,1)S(1)}, u32[]{:S(2)}, u32[]{:S(2)}) collective-permute-start(bf16[4,2,64,256]{3,2,1,0:T(8,128)(2,1)S(1)} %slice.384), channel_id=1, source_target_pairs={{256,0},{257,1},{258,2},{259,3},{260,4},{261,5},{262,6},{263,7},{2... | collective-permute-start | bytes 786440 | tf_op jit(solution)/shard_map/ppermute | solution.py:13
  89.5 8.5 %collective-permute-done.8 = bf16[4,2,64,256]{3,2,1,0:T(8,128)(2,1)S(1)} collective-permute-done((bf16[4,2,64,256]{3,2,1,0:T(8,128)(2,1)S(1)}, bf16[4,2,64,256]{3,2,1,0:T(8,128)(2,1)S(1)}, u32[]{:S(2)}, u32[]{:S(2)}) %collective-permute-start.8) | collective-permute-done | bytes 262176 | tf_op jit(solution)/shard_map/ppermute | solution.py:13
  98.0 0.7 slice_select_fusion.2
  (174 shorter events, 9.9 us)
Async XLA Ops:
  1.0 22.7 %collective-permute-start = (bf16[8,2,16,256]{3,2,1,0:T(8,128)(2,1)S(1)}, bf16[8,2,16,256]{3,2,1,0:T(8,128)(2,1)S(1)}, u32[]{:S(2)}, u32[]{:S(2)}) collective-permute-start(bf16[8,2,16,256]{3,2,1,0:T(8,128)(2,1)S(1)} %get-tuple-element.12), channel_id=1, source_target_pairs={{0,8},{8,16},{16,24},{24,32},{32,40},{40,48},{48,56},{56,64},{64,7... | collective-permute-start | bytes 393224 | tf_op jit(solution)/shard_map/ppermute | solution.py:24
  8.3 15.3 %collective-permute-start.5 = (bf16[16]{0:T(256)(128)(2,1)S(1)}, bf16[16]{0:T(256)(128)(2,1)S(1)}, u32[]{:S(2)}, u32[]{:S(2)}) collective-permute-start(bf16[16]{0:T(256)(128)(2,1)S(1)} %get-tuple-element.23), channel_id=1, source_target_pairs={{0,8},{8,16},{16,24},{24,32},{32,40},{40,48},{48,56},{56,64},{64,7... | collective-permute-start | bytes 104 | tf_op jit(solution)/shard_map/ppermute | solution.py:13
  12.1 11.5 %collective-permute-start.7 = (bf16[16]{0:T(256)(128)(2,1)S(1)}, bf16[16]{0:T(256)(128)(2,1)S(1)}, u32[]{:S(2)}, u32[]{:S(2)}) collective-permute-start(bf16[16]{0:T(256)(128)(2,1)S(1)} %get-tuple-element.24), channel_id=1, source_target_pairs={{8,0},{16,8},{24,16},{32,24},{40,32},{48,40},{56,48},{64,56},{72,6... | collective-permute-start | bytes 104 | tf_op jit(solution)/shard_map/ppermute | solution.py:13
  19.7 6.9 %collective-permute-start.1 = (bf16[8,2,16,256]{3,2,1,0:T(8,128)(2,1)S(1)}, bf16[8,2,16,256]{3,2,1,0:T(8,128)(2,1)S(1)}, u32[]{:S(2)}, u32[]{:S(2)}) collective-permute-start(bf16[8,2,16,256]{3,2,1,0:T(8,128)(2,1)S(1)} %get-tuple-element.11), channel_id=1, source_target_pairs={{8,0},{16,8},{24,16},{32,24},{40,32},{48,40},{56,48},{64,56},{72,6... | collective-permute-start | bytes 393224 | tf_op jit(solution)/shard_map/ppermute | solution.py:26
  27.9 1.7 %copy-start = (bf16[1,2,2304,256]{3,2,1,0:T(8,128)(2,1)S(1)}, bf16[1,2,2304,256]{3,2,1,0:T(8,128)(2,1)}, u32[]{:S(2)}) copy-start(bf16[1,2,2304,256]{3,2,1,0:T(8,128)(2,1)} %param.6) | copy-start | bytes 7077892
  29.6 1.1 %copy-start.6 = (bf16[1,2,768,256]{3,2,1,0:T(8,128)(2,1)S(1)}, bf16[1,2,768,256]{3,2,1,0:T(8,128)(2,1)}, u32[]{:S(2)}) copy-start(bf16[1,2,768,256]{3,2,1,0:T(8,128)(2,1)} %param.7) | copy-start | bytes 2359300
  32.4 1.7 %copy-start.1 = (bf16[1,2,2304,256]{3,2,1,0:T(8,128)(2,1)S(1)}, bf16[1,2,2304,256]{3,2,1,0:T(8,128)(2,1)}, u32[]{:S(2)}) copy-start(bf16[1,2,2304,256]{3,2,1,0:T(8,128)(2,1)} %param.6) | copy-start | bytes 7077892
  35.7 11.3 %collective-permute-start.2 = (bf16[4,2,96,256]{3,2,1,0:T(8,128)(2,1)S(1)}, bf16[4,2,96,256]{3,2,1,0:T(8,128)(2,1)S(1)}, u32[]{:S(2)}, u32[]{:S(2)}) collective-permute-start(bf16[4,2,96,256]{3,2,1,0:T(8,128)(2,1)S(1)} %fusion), channel_id=1, source_target_pairs={{0,256},{1,257},{2,258},{3,259},{4,260},{5,261},{6,262},{7,263},{8... | collective-permute-start | bytes 1179656 | tf_op jit(solution)/shard_map/ppermute | solution.py:13
  48.3 1.7 %copy-start.2 = (bf16[1,2,2304,256]{3,2,1,0:T(8,128)(2,1)S(1)}, bf16[1,2,2304,256]{3,2,1,0:T(8,128)(2,1)}, u32[]{:S(2)}) copy-start(bf16[1,2,2304,256]{3,2,1,0:T(8,128)(2,1)} %param.6) | copy-start | bytes 7077892
  50.0 1.2 %copy-start.7 = (bf16[1,2,768,256]{3,2,1,0:T(8,128)(2,1)S(1)}, bf16[1,2,768,256]{3,2,1,0:T(8,128)(2,1)}, u32[]{:S(2)}) copy-start(bf16[1,2,768,256]{3,2,1,0:T(8,128)(2,1)} %param.7) | copy-start | bytes 2359300
  52.9 1.7 %copy-start.3 = (bf16[1,2,2304,256]{3,2,1,0:T(8,128)(2,1)S(1)}, bf16[1,2,2304,256]{3,2,1,0:T(8,128)(2,1)}, u32[]{:S(2)}) copy-start(bf16[1,2,2304,256]{3,2,1,0:T(8,128)(2,1)} %param.6) | copy-start | bytes 7077892
  54.5 1.1 %copy-start.8 = (bf16[1,2,768,256]{3,2,1,0:T(8,128)(2,1)S(1)}, bf16[1,2,768,256]{3,2,1,0:T(8,128)(2,1)}, u32[]{:S(2)}) copy-start(bf16[1,2,768,256]{3,2,1,0:T(8,128)(2,1)} %param.7) | copy-start | bytes 2359300
  56.2 11.9 %collective-permute-start.3 = (bf16[4,2,96,256]{3,2,1,0:T(8,128)(2,1)S(1)}, bf16[4,2,96,256]{3,2,1,0:T(8,128)(2,1)S(1)}, u32[]{:S(2)}, u32[]{:S(2)}) collective-permute-start(bf16[4,2,96,256]{3,2,1,0:T(8,128)(2,1)S(1)} %fusion.1), channel_id=1, source_target_pairs={{0,256},{1,257},{2,258},{3,259},{4,260},{5,261},{6,262},{7,263},{8... | collective-permute-start | bytes 1179656 | tf_op jit(solution)/shard_map/ppermute | solution.py:13
  69.4 1.7 %copy-start.4 = (bf16[1,2,2304,256]{3,2,1,0:T(8,128)(2,1)S(1)}, bf16[1,2,2304,256]{3,2,1,0:T(8,128)(2,1)}, u32[]{:S(2)}) copy-start(bf16[1,2,2304,256]{3,2,1,0:T(8,128)(2,1)} %param.6) | copy-start | bytes 7077892
  71.1 1.1 %copy-start.9 = (bf16[1,2,768,256]{3,2,1,0:T(8,128)(2,1)S(1)}, bf16[1,2,768,256]{3,2,1,0:T(8,128)(2,1)}, u32[]{:S(2)}) copy-start(bf16[1,2,768,256]{3,2,1,0:T(8,128)(2,1)} %param.7) | copy-start | bytes 2359300
  73.9 1.7 %copy-start.5 = (bf16[1,2,2304,256]{3,2,1,0:T(8,128)(2,1)S(1)}, bf16[1,2,2304,256]{3,2,1,0:T(8,128)(2,1)}, u32[]{:S(2)}) copy-start(bf16[1,2,2304,256]{3,2,1,0:T(8,128)(2,1)} %param.6) | copy-start | bytes 7077892
  75.6 1.1 %copy-start.10 = (bf16[1,2,768,256]{3,2,1,0:T(8,128)(2,1)S(1)}, bf16[1,2,768,256]{3,2,1,0:T(8,128)(2,1)}, u32[]{:S(2)}) copy-start(bf16[1,2,768,256]{3,2,1,0:T(8,128)(2,1)} %param.7) | copy-start | bytes 2359300
  77.3 9.0 %collective-permute-start.4 = (bf16[8,2,16,256]{3,2,1,0:T(8,128)(2,1)S(1)}, bf16[8,2,16,256]{3,2,1,0:T(8,128)(2,1)S(1)}, u32[]{:S(2)}, u32[]{:S(2)}) collective-permute-start(bf16[8,2,16,256]{3,2,1,0:T(8,128)(2,1)S(1)} %get-tuple-element.9), channel_id=1, source_target_pairs={{0,8},{8,16},{16,24},{24,32},{32,40},{40,48},{48,56},{56,64},{64,7... | collective-permute-start | bytes 393224 | tf_op jit(solution)/shard_map/ppermute | solution.py:13
  79.4 8.4 %collective-permute-start.6 = (bf16[8,2,16,256]{3,2,1,0:T(8,128)(2,1)S(1)}, bf16[8,2,16,256]{3,2,1,0:T(8,128)(2,1)S(1)}, u32[]{:S(2)}, u32[]{:S(2)}) collective-permute-start(bf16[8,2,16,256]{3,2,1,0:T(8,128)(2,1)S(1)} %get-tuple-element.10), channel_id=1, source_target_pairs={{8,0},{16,8},{24,16},{32,24},{40,32},{48,40},{56,48},{64,56},{72,6... | collective-permute-start | bytes 393224 | tf_op jit(solution)/shard_map/ppermute | solution.py:13
  88.2 9.8 %collective-permute-start.8 = (bf16[4,2,64,256]{3,2,1,0:T(8,128)(2,1)S(1)}, bf16[4,2,64,256]{3,2,1,0:T(8,128)(2,1)S(1)}, u32[]{:S(2)}, u32[]{:S(2)}) collective-permute-start(bf16[4,2,64,256]{3,2,1,0:T(8,128)(2,1)S(1)} %slice.384), channel_id=1, source_target_pairs={{256,0},{257,1},{258,2},{259,3},{260,4},{261,5},{262,6},{263,7},{2... | collective-permute-start | bytes 786440 | tf_op jit(solution)/shard_map/ppermute | solution.py:13
where the time goes:
time: 99.5 us; the launch traced here: 98.7 us
  starting transfers between devices  38.8 us (39%)
  waiting for transfers between devices  25.1 us (25%)
  local copies, waits for them, and re-layouts  15.4 us (15%)
  matrix products  9.37 us (9%)
  other arithmetic  7.46 us (7%)
  between operations  2.56 us (3%)
    ppermute x7, starting transfers between devices, passed_along(): lax.ppermute(value, axis, [(source, source + steps) for source in range(l...  31.1 us
    ppermute x7, waiting for transfers between devices, passed_along(): lax.ppermute(value, axis, [(source, source + steps) for source in range(l...  23.3 us
    unnamed x66, local copies, waits for them, and re-layouts  9.03 us
    dot_general x6, matrix products, spatial_conv(): product = jnp.dot(stacked, weight, preferred_element_type=jnp.float32)  6.46 us
    ppermute x1, starting transfers between devices, padded_2(): lax.ppermute(head, axis, [((i + 1) % count, i) for i in range(ends)])  3.92 us
    ppermute x1, starting transfers between devices, padded_2(): lax.ppermute(tail, axis, [(i, (i + 1) % count) for i in range(ends)])  3.83 us
    dot_general x6, matrix products, temporal_conv(): jnp.dot(stacked.reshape(-1, stacked.shape[-1]), weight, preferred_element...  2.91 us
  transfers between devices with their start and end apart: 9, of which 6 were waited for; matrix products, arithmetic and copies ran while one was open for 4% of the time, Pallas kernels for 0%

commit v1 on v0

v1 whole, which is shorter than its diff:
```python
import functools

import jax
import jax.numpy as jnp
from jax import lax
from jax.experimental import pallas as pl
from jax.experimental.pallas import tpu as pltpu
from jax.sharding import PartitionSpec as P

MARGIN = 16
LANES = 128
GROUP = 2
EPSILON = 1e-6
MESH = pl.DeviceIdType.MESH


def norm_act(hbuf, sbuf):
    frames, rows, columns, channels = hbuf.shape
    count = rows * columns
    halves = channels // LANES
    row8 = lax.broadcasted_iota(jnp.int32, (8, LANES), 0)
    lane8 = lax.broadcasted_iota(jnp.int32, (8, LANES), 1)
    means = jnp.zeros((8, LANES), jnp.float32)
    squares = jnp.zeros((8, LANES), jnp.float32)
    for f in range(frames):
        for h in range(halves):
            x = hbuf[f, :, :, h * LANES : (h + 1) * LANES].reshape(count, LANES)
            mean = jnp.sum(x, axis=0, keepdims=True) * (1.0 / count)
            d = x - mean
            square = jnp.sum(d * d, axis=0, keepdims=True)
            here = row8 == f * halves + h
            means = jnp.where(here, mean, means)
            squares = jnp.where(here, square, squares)
    size = float(count)
    for step in (1, 2, 4):
        low = (lane8 & step) == 0
        mean2 = jnp.where(low, pltpu.roll(means, LANES - step, 1), pltpu.roll(means, step, 1))
        square2 = jnp.where(low, pltpu.roll(squares, LANES - step, 1), pltpu.roll(squares, step, 1))
        d = means - mean2
        squares = squares + square2 + d * d * (0.5 * size)
        means = (means + mean2) * 0.5
        size = 2.0 * size
    scale = lax.rsqrt(squares * (1.0 / size) + EPSILON)
    column = lax.broadcasted_iota(jnp.int32, (columns, LANES), 0)
    for f in range(frames):
        for h in range(halves):
            at = f * halves + h
            mean = means[at : at + 1, :]
            inv = scale[at : at + 1, :]
            for r in range(rows):
                y = (hbuf[f, r, :, h * LANES : (h + 1) * LANES] - mean) * inv
                half = 0.5 * y
                a = half * jnp.tanh(half) + half
                before = jnp.where(column == 0, 0.0, pltpu.roll(a, 1, 0))
                after = jnp.where(column == columns - 1, 0.0, pltpu.roll(a, columns - 1, 0))
                for b, piece in enumerate((before, a, after)):
                    lane = (r * 3 + b) * channels + h * LANES
                    sbuf[f * columns : (f + 1) * columns, lane : lane + LANES] = piece.astype(jnp.bfloat16)


def kernel(
    tiles, frames, sw_hbm, tw_hbm, ramp, inter, out,
    xbuf, obuf, spat, hbuf, sbuf, sw, tw, wown, wtile, wleft, wright, mleft, mright, bbuf,
    own_sem, load_sem, halo_send, halo_recv, fwd_send, fwd_recv,
    wt_send, wt_recv, mg_send, mg_recv, ret_send, ret_recv,
):
    seg = lax.axis_index("segment")
    place = lax.axis_index("tile")
    stream = lax.axis_index("stream")
    total, rows, columns, channels = xbuf.shape
    owned = columns - 2 * MARGIN
    groups = total // GROUP
    half = groups // 2
    far = lax.rem(place + tiles // 2, tiles)
    left = lax.rem(place + tiles - 1, tiles)
    right = lax.rem(place + 1, tiles)
    tile = jnp.where(seg == 0, place, far)
    first, last = seg == 0, seg == 1

    def loads(k):
        return (
            pltpu.make_async_copy(sw_hbm.at[0, k], sw.at[k], load_sem.at[2 * k]),
            pltpu.make_async_copy(tw_hbm.at[0, k], tw.at[k], load_sem.at[2 * k + 1]),
        )

    def own(g):
        at = pl.ds(g * GROUP, GROUP)
        return pltpu.make_async_copy(
            frames.at[at], xbuf.at[at, :, MARGIN : MARGIN + owned, :], own_sem.at[g]
        )

    def remote(src, dst, send, recv, where):
        return pltpu.make_async_remote_copy(
            src_ref=src, dst_ref=dst, send_sem=send, recv_sem=recv, device_id=where, device_id_type=MESH
        )

    def halos(g):
        at = pl.ds(g * GROUP, GROUP)
        return (
            remote(
                frames.at[at, :, owned - MARGIN : owned, :], xbuf.at[at, :, 0:MARGIN, :],
                halo_send.at[0, g], halo_recv.at[0, g], (seg, right, stream),
            ),
            remote(
                frames.at[at, :, 0:MARGIN, :], xbuf.at[at, :, MARGIN + owned : columns, :],
                halo_send.at[1, g], halo_recv.at[1, g], (seg, left, stream),
            ),
        )

    def forward(g):
        at = pl.ds(g * GROUP, GROUP)
        return remote(obuf.at[at], xbuf.at[at], fwd_send.at[g], fwd_recv.at[g], (1 - seg, far, stream))

    def weight_over():
        return remote(wown, wtile, wt_send.at[0], wt_recv.at[0], (1 - seg, far, stream))

    def weight_sides():
        return (
            remote(wtile.at[0:MARGIN], wright, wt_send.at[1], wt_recv.at[1], (seg, left, stream)),
            remote(wtile.at[columns - MARGIN : columns], wleft, wt_send.at[2], wt_recv.at[2], (seg, right, stream)),
        )

    def margins(g):
        at = pl.ds(g * GROUP, GROUP)
        return (
            remote(
                obuf.at[at, :, 0:MARGIN, :], mright.at[at],
                mg_send.at[0, g], mg_recv.at[0, g], (seg, left, stream),
            ),
            remote(
                obuf.at[at, :, columns - MARGIN : columns, :], mleft.at[at],
                mg_send.at[1, g], mg_recv.at[1, g], (seg, right, stream),
            ),
        )

    def give(g):
        to = g // half
        place_in = g % half
        return remote(
            bbuf.at[pl.ds(g * GROUP, GROUP)], out.at[pl.ds(place_in * GROUP, GROUP)],
            ret_send.at[g], ret_recv.at[place_in], (to, far, stream),
        )

    for k in range(2):
        for copy in loads(k):
            copy.start()

    @pl.when(first)
    def _():
        for g in range(groups):
            own(g).start()

    barrier = pltpu.get_barrier_semaphore()
    for where in ((seg, left, stream), (seg, right, stream), (1 - seg, far, stream)):
        pl.semaphore_signal(barrier, inc=1, device_id=where, device_id_type=MESH)

    @pl.when(last)
    def _():
        pl.semaphore_signal(barrier, inc=1, device_id=(seg, far, stream), device_id_type=MESH)

    pl.semaphore_wait(barrier, 3 + seg)

    @pl.when(first)
    def _():
        for g in range(groups):
            for copy in halos(g):
                copy.start()
        eye = lax.broadcasted_iota(jnp.int32, (columns, columns), 0) == lax.broadcasted_iota(
            jnp.int32, (columns, columns), 1
        )
        spread = jnp.where(eye, ramp[...].astype(jnp.float32), 0.0)
        weight = jnp.broadcast_to(jnp.sum(spread, axis=1, keepdims=True), (columns, LANES))
        position = lax.broadcasted_iota(jnp.int32, (columns, LANES), 0)
        inside = (position >= MARGIN - inter[0, 0]) & (position < MARGIN + owned + inter[0, 1])
        wown[...] = jnp.where(inside, weight, 0.0).astype(jnp.bfloat16)
        weight_over().start()

    for k in range(2):
        spat[k, 0:2] = jnp.zeros((2, rows, columns, channels), jnp.bfloat16)

    @pl.when(last)
    def _():
        weight_over().wait_recv()
        for copy in weight_sides():
            copy.start()

    def conv(k, g):
        norm_act(hbuf, sbuf)
        taps = 2 * 3 * channels
        act = sbuf[...]
        for r in range(rows):
            low = (1 - r) * 3 * channels
            product = jnp.dot(act, sw[k, low : low + taps, :], preferred_element_type=jnp.float32)
            spat[k, pl.ds(g * GROUP + 2, GROUP), r] = product.reshape(GROUP, columns, channels).astype(jnp.bfloat16)
        pieces = [
            spat[k, pl.ds(g * GROUP + q, GROUP)].reshape(GROUP * rows * columns, channels) for q in range(3)
        ]
        product = jnp.dot(jnp.concatenate(pieces, axis=-1), tw[k], preferred_element_type=jnp.float32)
        return product.reshape(GROUP, rows, columns, channels)

    def blend(g):
        for copy in margins(g):
            copy.wait_recv()
        own_w = wtile[MARGIN : MARGIN + owned, :].astype(jnp.float32)
        left_w = wleft[...].astype(jnp.float32) * (tile > 0).astype(jnp.float32)
        right_w = wright[...].astype(jnp.float32) * (tile < tiles - 1).astype(jnp.float32)
        parts = ((0, MARGIN, left_w, mleft), (MARGIN, owned - MARGIN, None, None), (owned - MARGIN, owned, right_w, mright))
        for low, high, side_w, side in parts:
            w = own_w[low:high]
            inv = 1.0 / (w if side is None else w + side_w)
            for f in range(GROUP):
                frame = g * GROUP + f
                for r in range(rows):
                    for h in range(channels // LANES):
                        lanes = slice(h * LANES, (h + 1) * LANES)
                        total_term = obuf[frame, r, MARGIN + low : MARGIN + high, lanes].astype(jnp.float32) * w
                        if side is not None:
                            total_term = total_term + side[frame, r, :, lanes].astype(jnp.float32) * side_w
                        bbuf[frame, r, low:high, lanes] = (total_term * inv).astype(jnp.bfloat16)
        give(g).start()

    def step(g):
        at = pl.ds(g * GROUP, GROUP)

        @pl.when(first)
        def _():
            own(g).wait()
            for copy in halos(g):
                copy.wait_recv()

            @pl.when(tile == 0)
            def _():
                xbuf[at, :, 0:MARGIN, :] = jnp.zeros((GROUP, rows, MARGIN, channels), jnp.bfloat16)

            @pl.when(tile == tiles - 1)
            def _():
                xbuf[at, :, MARGIN + owned : columns, :] = jnp.zeros((GROUP, rows, MARGIN, channels), jnp.bfloat16)

        @pl.when(last)
        def _():
            forward(g).wait_recv()

        hbuf[...] = xbuf[at].astype(jnp.float32)

        if g == 0:
            for copy in loads(0):
                copy.wait()

        hbuf[...] = conv(0, g)

        if g == 0:
            for copy in loads(1):
                copy.wait()

        obuf[at] = (xbuf[at].astype(jnp.float32) + conv(1, g)).astype(jnp.bfloat16)

        @pl.when(first)
        def _():
            forward(g).start()

        @pl.when(last)
        def _():
            for copy in margins(g):
                copy.start()

            if g == 0:
                for copy in weight_sides():
                    copy.wait_recv()
            else:
                blend(g - 1)

    for g in range(groups):
        step(g)

    @pl.when(last)
    def _():
        blend(groups - 1)
        for copy in weight_sides():
            copy.wait_send()
        for g in range(groups):
            for copy in margins(g):
                copy.wait_send()
            give(g).wait_send()

    @pl.when(first)
    def _():
        weight_over().wait_send()
        for g in range(groups):
            for copy in halos(g):
                copy.wait_send()
            forward(g).wait_send()

    for g in range(half):
        give(g).wait_recv()


def body(tiles, frames, spatial_weight, temporal_weight, ramp, intersection):
    total, rows, owned, channels = frames.shape
    columns = owned + 2 * MARGIN
    groups = total // GROUP
    bf16, f32 = jnp.bfloat16, jnp.float32
    dma = pltpu.SemaphoreType.DMA
    return pl.pallas_call(
        functools.partial(kernel, tiles),
        out_shape=jax.ShapeDtypeStruct((total // 2, rows, owned, channels), bf16),
        in_specs=[
            pl.BlockSpec(memory_space=pl.ANY),
            pl.BlockSpec(memory_space=pl.ANY),
            pl.BlockSpec(memory_space=pl.ANY),
            pl.BlockSpec(memory_space=pltpu.VMEM),
            pl.BlockSpec(memory_space=pltpu.SMEM),
        ],
        out_specs=pl.BlockSpec(memory_space=pl.ANY),
        scratch_shapes=[
            pltpu.VMEM((total, rows, columns, channels), bf16),
            pltpu.VMEM((total, rows, columns, channels), bf16),
            pltpu.VMEM((2, total + 2, rows, columns, channels), bf16),
            pltpu.VMEM((GROUP, rows, columns, channels), f32),
            pltpu.VMEM((GROUP * columns, rows * 3 * channels), bf16),
            pltpu.VMEM(spatial_weight.shape[1:], bf16),
            pltpu.VMEM(temporal_weight.shape[1:], bf16),
            pltpu.VMEM((columns, LANES), bf16),
            pltpu.VMEM((columns, LANES), bf16),
            pltpu.VMEM((MARGIN, LANES), bf16),
            pltpu.VMEM((MARGIN, LANES), bf16),
            pltpu.VMEM((total, rows, MARGIN, channels), bf16),
            pltpu.VMEM((total, rows, MARGIN, channels), bf16),
            pltpu.VMEM((total, rows, owned, channels), bf16),
            dma((groups,)),
            dma((4,)),
            dma((2, groups)),
            dma((2, groups)),
            dma((groups,)),
            dma((groups,)),
            dma((3,)),
            dma((3,)),
            dma((2, groups)),
            dma((2, groups)),
            dma((groups,)),
            dma((groups // 2,)),
        ],
        compiler_params=pltpu.CompilerParams(
            collective_id=0, has_side_effects=True, vmem_limit_bytes=48 * 1024 * 1024
        ),
    )(frames, spatial_weight, temporal_weight, ramp, intersection)


def solution(mesh):
    in_specs = (
        P(None, "stream", "tile", None),
        P("segment", None, None, None),
        P("segment", None, None, None),
        P("tile", None),
        P("tile", None),
    )
    out_specs = P("segment", "stream", "tile", None)
    return jax.shard_map(
        functools.partial(body, mesh.shape["tile"]),
        mesh=mesh, in_specs=in_specs, out_specs=out_specs, check_vma=False,
    )
```

time: 99.5 us -> 52.7 us (0.53)
  the two profiles are of different devices: /device:TPU:26 before, /device:TPU:20 now
where the time goes in v1:
time: 52.7 us; the launch traced here: 52.4 us
  Pallas kernels  46.6 us (88%)
  local copies, waits for them, and re-layouts  5.85 us (11%)
    pallas_call x1, Pallas kernels, body(): pl.pallas_call(functools.partial(kernel, tiles), out_shape=jax.ShapeDtype...  46.6 us
    unnamed x11, local copies, waits for them, and re-layouts  5.85 us

profile of v1, /device:TPU:20, one launch (start us, length us, event | category | flops | bytes accessed | tf_op | source)
XLA Modules:
  0.0 52.4 jit_solution(3856110978820262627)
XLA Ops:
  0.0 0.0 copy-start
  0.0 1.7 %copy-done = bf16[1,2,2304,256]{3,2,1,0:T(8,128)(2,1)S(1)} copy-done((bf16[1,2,2304,256]{3,2,1,0:T(8,128)(2,1)S(1)}, bf16[1,2,2304,256]{3,2,1,0:T(8,128)(2,1)}, u32[]{:S(2)}) %copy-start) | copy-done | bytes 2359320
  1.7 0.0 copy-start.1
  1.7 1.1 %copy-done.1 = bf16[1,2,768,256]{3,2,1,0:T(8,128)(2,1)S(1)} copy-done((bf16[1,2,768,256]{3,2,1,0:T(8,128)(2,1)S(1)}, bf16[1,2,768,256]{3,2,1,0:T(8,128)(2,1)}, u32[]{:S(2)}) %copy-start.1) | copy-done | bytes 786456
  2.8 0.0 copy-start.2
  2.8 1.0 %copy-done.2 = bf16[8,2,64,256]{3,2,1,0:T(8,128)(2,1)S(1)} copy-done((bf16[8,2,64,256]{3,2,1,0:T(8,128)(2,1)S(1)}, bf16[8,2,64,256]{3,2,1,0:T(8,128)(2,1)}, u32[]{:S(2)}) %copy-start.2) | copy-done | bytes 524312
  3.8 0.0 copy-start.3
  3.8 0.7 %copy-done.3 = s32[1,96]{1,0:T(1,128)S(1)} copy-done((s32[1,96]{1,0:T(1,128)S(1)}, s32[1,96]{1,0:T(1,128)}, u32[]{:S(2)}) %copy-start.3) | copy-done | bytes 408
  4.5 0.0 copy-start.4
  4.5 0.7 %copy-done.4 = s32[1,2]{1,0:T(1,128)S(1)} copy-done((s32[1,2]{1,0:T(1,128)S(1)}, s32[1,2]{1,0:T(1,128)}, u32[]{:S(2)}) %copy-start.4) | copy-done | bytes 32
  5.2 46.6 %shard_map.55 = bf16[4,2,64,256]{3,2,1,0:T(8,128)(2,1)S(1)} custom-call(bf16[8,2,64,256]{3,2,1,0:T(8,128)(2,1)S(1)} %copy-done.2, bf16[1,2,2304,256]{3,2,1,0:T(8,128)(2,1)S(1)} %copy-done, bf16[1,2,768,256]{3,2,1,0:T(8,128)(2,1)S(1)} %copy-done.1, s32[1,96]{1,0:T(1,128)S(1)} %copy-done.3, s32[1,2]{1,0:T(1,128)S(1)} %copy-done.4), custom_call_target="tpu_custom_call" | custom-call | tf_op jit(solution)/shard_map/pallas_call | solution.py:303
  51.7 0.7 %copy.7 = bf16[4,2,64,256]{3,2,1,0:T(8,128)(2,1)} copy(bf16[4,2,64,256]{3,2,1,0:T(8,128)(2,1)S(1)} %shard_map.55) | data formatting | bytes 524288
Async XLA Ops:
  0.0 1.7 %copy-start = (bf16[1,2,2304,256]{3,2,1,0:T(8,128)(2,1)S(1)}, bf16[1,2,2304,256]{3,2,1,0:T(8,128)(2,1)}, u32[]{:S(2)}) copy-start(bf16[1,2,2304,256]{3,2,1,0:T(8,128)(2,1)} %sw_hbm.1) | copy-start | bytes 7077892
  1.7 1.1 %copy-start.1 = (bf16[1,2,768,256]{3,2,1,0:T(8,128)(2,1)S(1)}, bf16[1,2,768,256]{3,2,1,0:T(8,128)(2,1)}, u32[]{:S(2)}) copy-start(bf16[1,2,768,256]{3,2,1,0:T(8,128)(2,1)} %tw_hbm.1) | copy-start | bytes 2359300
  2.8 1.0 %copy-start.2 = (bf16[8,2,64,256]{3,2,1,0:T(8,128)(2,1)S(1)}, bf16[8,2,64,256]{3,2,1,0:T(8,128)(2,1)}, u32[]{:S(2)}) copy-start(bf16[8,2,64,256]{3,2,1,0:T(8,128)(2,1)} %frames.1) | copy-start | bytes 1572868
  3.8 0.7 %copy-start.3 = (s32[1,96]{1,0:T(1,128)S(1)}, s32[1,96]{1,0:T(1,128)}, u32[]{:S(2)}) copy-start(s32[1,96]{1,0:T(1,128)} %ramp.1) | copy-start | bytes 1156
  4.5 0.7 %copy-start.4 = (s32[1,2]{1,0:T(1,128)S(1)}, s32[1,2]{1,0:T(1,128)}, u32[]{:S(2)}) copy-start(s32[1,2]{1,0:T(1,128)} %inter.1) | copy-start | bytes 28

commit v2 on v1

--- a/solution.py
+++ b/solution.py
@@ -304,13 +304,13 @@
         functools.partial(kernel, tiles),
         out_shape=jax.ShapeDtypeStruct((total // 2, rows, owned, channels), bf16),
         in_specs=[
-            pl.BlockSpec(memory_space=pl.ANY),
-            pl.BlockSpec(memory_space=pl.ANY),
-            pl.BlockSpec(memory_space=pl.ANY),
+            pl.BlockSpec(memory_space=pltpu.HBM),
+            pl.BlockSpec(memory_space=pltpu.HBM),
+            pl.BlockSpec(memory_space=pltpu.HBM),
             pl.BlockSpec(memory_space=pltpu.VMEM),
             pl.BlockSpec(memory_space=pltpu.SMEM),
         ],
-        out_specs=pl.BlockSpec(memory_space=pl.ANY),
+        out_specs=pl.BlockSpec(memory_space=pltpu.HBM),
         scratch_shapes=[
             pltpu.VMEM((total, rows, columns, channels), bf16),
             pltpu.VMEM((total, rows, columns, channels), bf16),
@@ -340,7 +340,7 @@
             dma((groups // 2,)),
         ],
         compiler_params=pltpu.CompilerParams(
-            collective_id=0, has_side_effects=True, vmem_limit_bytes=48 * 1024 * 1024
+            collective_id=0, has_side_effects=True, vmem_limit_bytes=60 * 1024 * 1024
         ),
     )(frames, spatial_weight, temporal_weight, ramp, intersection)
 

time: 52.7 us -> 48 us (0.911)
  the two profiles are of different devices: /device:TPU:20 before, /device:TPU:12 now
where the time goes in v2:
time: 48 us; the launch traced here: 47.8 us
  Pallas kernels  46.2 us (96%)
  local copies, waits for them, and re-layouts  1.67 us (3%)
    pallas_call x1, Pallas kernels, body(): pl.pallas_call(functools.partial(kernel, tiles), out_shape=jax.ShapeDtype...  46.2 us
    unnamed x1, local copies, waits for them, and re-layouts  1.67 us

profile of v2, /device:TPU:12, one launch (start us, length us, event | category | flops | bytes accessed | tf_op | source)
XLA Modules:
  0.0 47.8 jit_solution(4494786325630863653)
XLA Ops:
  0.0 46.2 %shard_map.55 = bf16[4,2,64,256]{3,2,1,0:T(8,128)(2,1)} custom-call(bf16[8,2,64,256]{3,2,1,0:T(8,128)(2,1)} %frames.1, bf16[1,2,2304,256]{3,2,1,0:T(8,128)(2,1)} %sw_hbm.1, bf16[1,2,768,256]{3,2,1,0:T(8,128)(2,1)} %tw_hbm.1, s32[1,96]{1,0:T(1,128)} %ramp.1, s32[1,2]{1,0:T(1,128)} %inter.1), custom_call_target="tpu_custom_call" | custom-call | tf_op jit(solution)/shard_map/pallas_call | solution.py:303
  46.2 1.7 %copy.7 = bf16[4,2,64,256]{3,2,1,0:T(8,128)(2,1)} copy(bf16[4,2,64,256]{3,2,1,0:T(8,128)(2,1)} %shard_map.55) | data formatting | bytes 524288

commit v3 on v2

--- a/solution.py
+++ b/solution.py
@@ -9,7 +9,7 @@
 
 MARGIN = 16
 LANES = 128
-GROUP = 2
+GROUP = 1
 EPSILON = 1e-6
 MESH = pl.DeviceIdType.MESH
 
@@ -60,7 +60,7 @@
 
 def kernel(
     tiles, frames, sw_hbm, tw_hbm, ramp, inter, out,
-    xbuf, obuf, spat, hbuf, sbuf, sw, tw, wown, wtile, wleft, wright, mleft, mright, bbuf,
+    xbuf, obuf, spat, hbuf, sbuf, sw, tw, wtile, wleft, wright, mleft, mright, bbuf,
     own_sem, load_sem, halo_send, halo_recv, fwd_send, fwd_recv,
     wt_send, wt_recv, mg_send, mg_recv, ret_send, ret_recv,
 ):
@@ -71,10 +71,8 @@
     owned = columns - 2 * MARGIN
     groups = total // GROUP
     half = groups // 2
-    far = lax.rem(place + tiles // 2, tiles)
     left = lax.rem(place + tiles - 1, tiles)
     right = lax.rem(place + 1, tiles)
-    tile = jnp.where(seg == 0, place, far)
     first, last = seg == 0, seg == 1
 
     def loads(k):
@@ -109,15 +107,12 @@
 
     def forward(g):
         at = pl.ds(g * GROUP, GROUP)
-        return remote(obuf.at[at], xbuf.at[at], fwd_send.at[g], fwd_recv.at[g], (1 - seg, far, stream))
-
-    def weight_over():
-        return remote(wown, wtile, wt_send.at[0], wt_recv.at[0], (1 - seg, far, stream))
+        return remote(obuf.at[at], xbuf.at[at], fwd_send.at[g], fwd_recv.at[g], (1 - seg, place, stream))
 
     def weight_sides():
         return (
-            remote(wtile.at[0:MARGIN], wright, wt_send.at[1], wt_recv.at[1], (seg, left, stream)),
-            remote(wtile.at[columns - MARGIN : columns], wleft, wt_send.at[2], wt_recv.at[2], (seg, right, stream)),
+            remote(wtile.at[0:MARGIN], wright, wt_send.at[0], wt_recv.at[0], (seg, left, stream)),
+            remote(wtile.at[columns - MARGIN : columns], wleft, wt_send.at[1], wt_recv.at[1], (seg, right, stream)),
         )
 
     def margins(g):
@@ -134,37 +129,41 @@
         )
 
     def give(g):
-        to = g // half
-        place_in = g % half
-        return remote(
-            bbuf.at[pl.ds(g * GROUP, GROUP)], out.at[pl.ds(place_in * GROUP, GROUP)],
-            ret_send.at[g], ret_recv.at[place_in], (to, far, stream),
-        )
-
-    for k in range(2):
-        for copy in loads(k):
-            copy.start()
+        at = pl.ds(g % half * GROUP, GROUP)
+        src = bbuf.at[pl.ds(g * GROUP, GROUP)]
+        if g < half:
+            return remote(src, out.at[at], ret_send.at[g], ret_recv.at[g], (1 - seg, place, stream))
+        return pltpu.make_async_copy(src, out.at[at], ret_send.at[g])
+
+    barrier = pltpu.get_barrier_semaphore()
+    for where in ((seg, left, stream), (seg, right, stream), (1 - seg, place, stream)):
+        pl.semaphore_signal(barrier, inc=1, device_id=where, device_id_type=MESH)
 
     @pl.when(first)
     def _():
-        for g in range(groups):
+        own(0).start()
+
+    for copy in loads(0):
+        copy.start()
+
+    @pl.when(first)
+    def _():
+        for g in range(1, groups):
             own(g).start()
 
-    barrier = pltpu.get_barrier_semaphore()
-    for where in ((seg, left, stream), (seg, right, stream), (1 - seg, far, stream)):
-        pl.semaphore_signal(barrier, inc=1, device_id=where, device_id_type=MESH)
-
-    @pl.when(last)
-    def _():
-        pl.semaphore_signal(barrier, inc=1, device_id=(seg, far, stream), device_id_type=MESH)
-
-    pl.semaphore_wait(barrier, 3 + seg)
+    for copy in loads(1):
+        copy.start()
+
+    pl.semaphore_wait(barrier, 3)
 
     @pl.when(first)
     def _():
         for g in range(groups):
             for copy in halos(g):
                 copy.start()
+
+    @pl.when(last)
+    def _():
         eye = lax.broadcasted_iota(jnp.int32, (columns, columns), 0) == lax.broadcasted_iota(
             jnp.int32, (columns, columns), 1
         )
@@ -172,17 +171,12 @@
         weight = jnp.broadcast_to(jnp.sum(spread, axis=1, keepdims=True), (columns, LANES))
         position = lax.broadcasted_iota(jnp.int32, (columns, LANES), 0)
         inside = (position >= MARGIN - inter[0, 0]) & (position < MARGIN + owned + inter[0, 1])
-        wown[...] = jnp.where(inside, weight, 0.0).astype(jnp.bfloat16)
-        weight_over().start()
+        wtile[...] = jnp.where(inside, weight, 0.0).astype(jnp.bfloat16)
+        for copy in weight_sides():
+            copy.start()
 
     for k in range(2):
         spat[k, 0:2] = jnp.zeros((2, rows, columns, channels), jnp.bfloat16)
-
-    @pl.when(last)
-    def _():
-        weight_over().wait_recv()
-        for copy in weight_sides():
-            copy.start()
 
     def conv(k, g):
         norm_act(hbuf, sbuf)
@@ -202,8 +196,8 @@
         for copy in margins(g):
             copy.wait_recv()
         own_w = wtile[MARGIN : MARGIN + owned, :].astype(jnp.float32)
-        left_w = wleft[...].astype(jnp.float32) * (tile > 0).astype(jnp.float32)
-        right_w = wright[...].astype(jnp.float32) * (tile < tiles - 1).astype(jnp.float32)
+        left_w = wleft[...].astype(jnp.float32) * (place > 0).astype(jnp.float32)
+        right_w = wright[...].astype(jnp.float32) * (place < tiles - 1).astype(jnp.float32)
         parts = ((0, MARGIN, left_w, mleft), (MARGIN, owned - MARGIN, None, None), (owned - MARGIN, owned, right_w, mright))
         for low, high, side_w, side in parts:
             w = own_w[low:high]
@@ -228,11 +222,11 @@
             for copy in halos(g):
                 copy.wait_recv()
 
-            @pl.when(tile == 0)
+            @pl.when(place == 0)
             def _():
                 xbuf[at, :, 0:MARGIN, :] = jnp.zeros((GROUP, rows, MARGIN, channels), jnp.bfloat16)
 
-            @pl.when(tile == tiles - 1)
+            @pl.when(place == tiles - 1)
             def _():
                 xbuf[at, :, MARGIN + owned : columns, :] = jnp.zeros((GROUP, rows, MARGIN, channels), jnp.bfloat16)
 
@@ -280,18 +274,19 @@
         for g in range(groups):
             for copy in margins(g):
                 copy.wait_send()
-            give(g).wait_send()
+            if g < half:
+                give(g).wait_send()
+            else:
+                give(g).wait()
 
     @pl.when(first)
     def _():
-        weight_over().wait_send()
         for g in range(groups):
             for copy in halos(g):
                 copy.wait_send()
             forward(g).wait_send()
-
-    for g in range(half):
-        give(g).wait_recv()
+        for g in range(half):
+            give(g).wait_recv()
 
 
 def body(tiles, frames, spatial_weight, temporal_weight, ramp, intersection):
@@ -310,7 +305,7 @@
             pl.BlockSpec(memory_space=pltpu.VMEM),
             pl.BlockSpec(memory_space=pltpu.SMEM),
         ],
-        out_specs=pl.BlockSpec(memory_space=pltpu.HBM),
+        out_specs=pl.BlockSpec(memory_space=pl.ANY),
         scratch_shapes=[
             pltpu.VMEM((total, rows, columns, channels), bf16),
             pltpu.VMEM((total, rows, columns, channels), bf16),
@@ -319,7 +314,6 @@
             pltpu.VMEM((GROUP * columns, rows * 3 * channels), bf16),
             pltpu.VMEM(spatial_weight.shape[1:], bf16),
             pltpu.VMEM(temporal_weight.shape[1:], bf16),
-            pltpu.VMEM((columns, LANES), bf16),
             pltpu.VMEM((columns, LANES), bf16),
             pltpu.VMEM((MARGIN, LANES), bf16),
             pltpu.VMEM((MARGIN, LANES), bf16),
@@ -332,15 +326,15 @@
             dma((2, groups)),
             dma((groups,)),
             dma((groups,)),
-            dma((3,)),
-            dma((3,)),
+            dma((2,)),
+            dma((2,)),
             dma((2, groups)),
             dma((2, groups)),
             dma((groups,)),
             dma((groups // 2,)),
         ],
         compiler_params=pltpu.CompilerParams(
-            collective_id=0, has_side_effects=True, vmem_limit_bytes=60 * 1024 * 1024
+            collective_id=0, has_side_effects=True, vmem_limit_bytes=56 * 1024 * 1024
         ),
     )(frames, spatial_weight, temporal_weight, ramp, intersection)
 

time: 48 us -> 50.4 us (1.050)
  the two profiles are of different devices: /device:TPU:12 before, /device:TPU:30 now
where the time goes in v3:
time: 50.4 us; the launch traced here: 50.2 us
  Pallas kernels  48.6 us (96%)
  local copies, waits for them, and re-layouts  1.67 us (3%)
    pallas_call x1, Pallas kernels, body(): pl.pallas_call(functools.partial(kernel, tiles), out_shape=jax.ShapeDtype...  48.6 us
    unnamed x1, local copies, waits for them, and re-layouts  1.67 us

profile of v3, /device:TPU:30, one launch (start us, length us, event | category | flops | bytes accessed | tf_op | source)
XLA Modules:
  0.0 50.2 jit_solution(1147471959872578933)
XLA Ops:
  0.0 48.6 %shard_map.55 = bf16[4,2,64,256]{3,2,1,0:T(8,128)(2,1)} custom-call(bf16[8,2,64,256]{3,2,1,0:T(8,128)(2,1)} %frames.1, bf16[1,2,2304,256]{3,2,1,0:T(8,128)(2,1)} %sw_hbm.1, bf16[1,2,768,256]{3,2,1,0:T(8,128)(2,1)} %tw_hbm.1, s32[1,96]{1,0:T(1,128)} %ramp.1, s32[1,2]{1,0:T(1,128)} %inter.1), custom_call_target="tpu_custom_call" | custom-call | tf_op jit(solution)/shard_map/pallas_call | solution.py:298
  48.6 1.7 %copy.7 = bf16[4,2,64,256]{3,2,1,0:T(8,128)(2,1)} copy(bf16[4,2,64,256]{3,2,1,0:T(8,128)(2,1)} %shard_map.55) | data formatting | bytes 524288

commit v4 on v3

--- a/solution.py
+++ b/solution.py
@@ -9,13 +9,14 @@
 
 MARGIN = 16
 LANES = 128
-GROUP = 1
+GROUPS = (2, 2, 2, 2)
+STARTS = (0, 2, 4, 6)
 EPSILON = 1e-6
 MESH = pl.DeviceIdType.MESH
 
 
-def norm_act(hbuf, sbuf):
-    frames, rows, columns, channels = hbuf.shape
+def norm_act(hbuf, sbuf, frames):
+    _, rows, columns, channels = hbuf.shape
     count = rows * columns
     halves = channels // LANES
     row8 = lax.broadcasted_iota(jnp.int32, (8, LANES), 0)
@@ -69,8 +70,8 @@
     stream = lax.axis_index("stream")
     total, rows, columns, channels = xbuf.shape
     owned = columns - 2 * MARGIN
-    groups = total // GROUP
-    half = groups // 2
+    groups = len(GROUPS)
+    half = STARTS.index(total // 2)
     left = lax.rem(place + tiles - 1, tiles)
     right = lax.rem(place + 1, tiles)
     first, last = seg == 0, seg == 1
@@ -82,7 +83,7 @@
         )
 
     def own(g):
-        at = pl.ds(g * GROUP, GROUP)
+        at = pl.ds(STARTS[g], GROUPS[g])
         return pltpu.make_async_copy(
             frames.at[at], xbuf.at[at, :, MARGIN : MARGIN + owned, :], own_sem.at[g]
         )
@@ -93,7 +94,7 @@
         )
 
     def halos(g):
-        at = pl.ds(g * GROUP, GROUP)
+        at = pl.ds(STARTS[g], GROUPS[g])
         return (
             remote(
                 frames.at[at, :, owned - MARGIN : owned, :], xbuf.at[at, :, 0:MARGIN, :],
@@ -106,7 +107,7 @@
         )
 
     def forward(g):
-        at = pl.ds(g * GROUP, GROUP)
+        at = pl.ds(STARTS[g], GROUPS[g])
         return remote(obuf.at[at], xbuf.at[at], fwd_send.at[g], fwd_recv.at[g], (1 - seg, place, stream))
 
     def weight_sides():
@@ -116,7 +117,7 @@
         )
 
     def margins(g):
-        at = pl.ds(g * GROUP, GROUP)
+        at = pl.ds(STARTS[g], GROUPS[g])
         return (
             remote(
                 obuf.at[at, :, 0:MARGIN, :], mright.at[at],
@@ -129,8 +130,8 @@
         )
 
     def give(g):
-        at = pl.ds(g % half * GROUP, GROUP)
-        src = bbuf.at[pl.ds(g * GROUP, GROUP)]
+        at = pl.ds(STARTS[g] % (total // 2), GROUPS[g])
+        src = bbuf.at[pl.ds(STARTS[g], GROUPS[g])]
         if g < half:
             return remote(src, out.at[at], ret_send.at[g], ret_recv.at[g], (1 - seg, place, stream))
         return pltpu.make_async_copy(src, out.at[at], ret_send.at[g])
@@ -179,18 +180,19 @@
         spat[k, 0:2] = jnp.zeros((2, rows, columns, channels), jnp.bfloat16)
 
     def conv(k, g):
-        norm_act(hbuf, sbuf)
+        size, start = GROUPS[g], STARTS[g]
+        norm_act(hbuf, sbuf, size)
         taps = 2 * 3 * channels
-        act = sbuf[...]
+        act = sbuf[0 : size * columns]
         for r in range(rows):
             low = (1 - r) * 3 * channels
             product = jnp.dot(act, sw[k, low : low + taps, :], preferred_element_type=jnp.float32)
-            spat[k, pl.ds(g * GROUP + 2, GROUP), r] = product.reshape(GROUP, columns, channels).astype(jnp.bfloat16)
+            spat[k, start + 2 : start + 2 + size, r] = product.reshape(size, columns, channels).astype(jnp.bfloat16)
         pieces = [
-            spat[k, pl.ds(g * GROUP + q, GROUP)].reshape(GROUP * rows * columns, channels) for q in range(3)
+            spat[k, start + q : start + q + size].reshape(size * rows * columns, channels) for q in range(3)
         ]
         product = jnp.dot(jnp.concatenate(pieces, axis=-1), tw[k], preferred_element_type=jnp.float32)
-        return product.reshape(GROUP, rows, columns, channels)
+        return product.reshape(size, rows, columns, channels)
 
     def blend(g):
         for copy in margins(g):
@@ -202,8 +204,7 @@
         for low, high, side_w, side in parts:
             w = own_w[low:high]
             inv = 1.0 / (w if side is None else w + side_w)
-            for f in range(GROUP):
-                frame = g * GROUP + f
+            for frame in range(STARTS[g], STARTS[g] + GROUPS[g]):
                 for r in range(rows):
                     for h in range(channels // LANES):
                         lanes = slice(h * LANES, (h + 1) * LANES)
@@ -214,7 +215,7 @@
         give(g).start()
 
     def step(g):
-        at = pl.ds(g * GROUP, GROUP)
+        at = pl.ds(STARTS[g], GROUPS[g])
 
         @pl.when(first)
         def _():
@@ -224,23 +225,23 @@
 
             @pl.when(place == 0)
             def _():
-                xbuf[at, :, 0:MARGIN, :] = jnp.zeros((GROUP, rows, MARGIN, channels), jnp.bfloat16)
+                xbuf[at, :, 0:MARGIN, :] = jnp.zeros((GROUPS[g], rows, MARGIN, channels), jnp.bfloat16)
 
             @pl.when(place == tiles - 1)
             def _():
-                xbuf[at, :, MARGIN + owned : columns, :] = jnp.zeros((GROUP, rows, MARGIN, channels), jnp.bfloat16)
+                xbuf[at, :, MARGIN + owned : columns, :] = jnp.zeros((GROUPS[g], rows, MARGIN, channels), jnp.bfloat16)
 
         @pl.when(last)
         def _():
             forward(g).wait_recv()
 
-        hbuf[...] = xbuf[at].astype(jnp.float32)
+        hbuf[0 : GROUPS[g]] = xbuf[at].astype(jnp.float32)
 
         if g == 0:
             for copy in loads(0):
                 copy.wait()
 
-        hbuf[...] = conv(0, g)
+        hbuf[0 : GROUPS[g]] = conv(0, g)
 
         if g == 0:
             for copy in loads(1):
@@ -292,12 +293,12 @@
 def body(tiles, frames, spatial_weight, temporal_weight, ramp, intersection):
     total, rows, owned, channels = frames.shape
     columns = owned + 2 * MARGIN
-    groups = total // GROUP
+    groups = len(GROUPS)
     bf16, f32 = jnp.bfloat16, jnp.float32
     dma = pltpu.SemaphoreType.DMA
     return pl.pallas_call(
         functools.partial(kernel, tiles),
-        out_shape=jax.ShapeDtypeStruct((total // 2, rows, owned, channels), bf16),
+        out_shape=pltpu.VMEM((total // 2, rows, owned, channels), bf16),
         in_specs=[
             pl.BlockSpec(memory_space=pltpu.HBM),
             pl.BlockSpec(memory_space=pltpu.HBM),
@@ -310,8 +311,8 @@
             pltpu.VMEM((total, rows, columns, channels), bf16),
             pltpu.VMEM((total, rows, columns, channels), bf16),
             pltpu.VMEM((2, total + 2, rows, columns, channels), bf16),
-            pltpu.VMEM((GROUP, rows, columns, channels), f32),
-            pltpu.VMEM((GROUP * columns, rows * 3 * channels), bf16),
+            pltpu.VMEM((max(GROUPS), rows, columns, channels), f32),
+            pltpu.VMEM((max(GROUPS) * columns, rows * 3 * channels), bf16),
             pltpu.VMEM(spatial_weight.shape[1:], bf16),
             pltpu.VMEM(temporal_weight.shape[1:], bf16),
             pltpu.VMEM((columns, LANES), bf16),
@@ -331,7 +332,7 @@
             dma((2, groups)),
             dma((2, groups)),
             dma((groups,)),
-            dma((groups // 2,)),
+            dma((STARTS.index(total // 2),)),
         ],
         compiler_params=pltpu.CompilerParams(
             collective_id=0, has_side_effects=True, vmem_limit_bytes=56 * 1024 * 1024

time: 50.4 us -> 44.1 us (0.88)
  Pallas kernels: 48.6 us -> 43.3 us
  local copies, waits for them, and re-layouts: 1.67 us -> 0.71 us
    pallas_call x1, Pallas kernels: 48.6 us -> 43.3 us  [body(): pl.pallas_call(functools.partial(kernel, tiles), out_shape=pltpu.VMEM((to...]
    unnamed x1, local copies, waits for them, and re-layouts: 1.67 us -> 0.71 us
where the time goes in v4:
time: 44.1 us; the launch traced here: 44 us
  Pallas kernels  43.3 us (98%)
  local copies, waits for them, and re-layouts  0.71 us (2%)
    pallas_call x1, Pallas kernels, body(): pl.pallas_call(functools.partial(kernel, tiles), out_shape=pltpu.VMEM((to...  43.3 us

profile of v4, /device:TPU:30, one launch (start us, length us, event | category | flops | bytes accessed | tf_op | source)
XLA Modules:
  0.0 44.0 jit_solution(16402356571323588118)
XLA Ops:
  0.0 43.3 %shard_map.55 = bf16[4,2,64,256]{3,2,1,0:T(8,128)(2,1)S(1)} custom-call(bf16[8,2,64,256]{3,2,1,0:T(8,128)(2,1)} %frames.1, bf16[1,2,2304,256]{3,2,1,0:T(8,128)(2,1)} %sw_hbm.1, bf16[1,2,768,256]{3,2,1,0:T(8,128)(2,1)} %tw_hbm.1, s32[1,96]{1,0:T(1,128)} %ramp.1, s32[1,2]{1,0:T(1,128)} %inter.1), custom_call_target="tpu_custom_call" | custom-call | tf_op jit(solution)/shard_map/pallas_call | solution.py:299
  43.3 0.7 %copy.7 = bf16[4,2,64,256]{3,2,1,0:T(8,128)(2,1)} copy(bf16[4,2,64,256]{3,2,1,0:T(8,128)(2,1)S(1)} %shard_map.55) | data formatting | bytes 524288

commit v5 on v4

--- a/solution.py
+++ b/solution.py
@@ -130,11 +130,8 @@
         )
 
     def give(g):
-        at = pl.ds(STARTS[g] % (total // 2), GROUPS[g])
-        src = bbuf.at[pl.ds(STARTS[g], GROUPS[g])]
-        if g < half:
-            return remote(src, out.at[at], ret_send.at[g], ret_recv.at[g], (1 - seg, place, stream))
-        return pltpu.make_async_copy(src, out.at[at], ret_send.at[g])
+        at = pl.ds(STARTS[g], GROUPS[g])
+        return remote(bbuf.at[at], out.at[at], ret_send.at[g], ret_recv.at[g], (1 - seg, place, stream))
 
     barrier = pltpu.get_barrier_semaphore()
     for where in ((seg, left, stream), (seg, right, stream), (1 - seg, place, stream)):
@@ -211,8 +208,10 @@
                         total_term = obuf[frame, r, MARGIN + low : MARGIN + high, lanes].astype(jnp.float32) * w
                         if side is not None:
                             total_term = total_term + side[frame, r, :, lanes].astype(jnp.float32) * side_w
-                        bbuf[frame, r, low:high, lanes] = (total_term * inv).astype(jnp.bfloat16)
-        give(g).start()
+                        target, row = (bbuf, frame) if g < half else (out, frame - total // 2)
+                        target[row, r, low:high, lanes] = (total_term * inv).astype(jnp.bfloat16)
+        if g < half:
+            give(g).start()
 
     def step(g):
         at = pl.ds(STARTS[g], GROUPS[g])
@@ -277,8 +276,6 @@
                 copy.wait_send()
             if g < half:
                 give(g).wait_send()
-            else:
-                give(g).wait()
 
     @pl.when(first)
     def _():
@@ -306,7 +303,7 @@
             pl.BlockSpec(memory_space=pltpu.VMEM),
             pl.BlockSpec(memory_space=pltpu.SMEM),
         ],
-        out_specs=pl.BlockSpec(memory_space=pl.ANY),
+        out_specs=pl.BlockSpec(memory_space=pltpu.VMEM),
         scratch_shapes=[
             pltpu.VMEM((total, rows, columns, channels), bf16),
             pltpu.VMEM((total, rows, columns, channels), bf16),
@@ -320,7 +317,7 @@
             pltpu.VMEM((MARGIN, LANES), bf16),
             pltpu.VMEM((total, rows, MARGIN, channels), bf16),
             pltpu.VMEM((total, rows, MARGIN, channels), bf16),
-            pltpu.VMEM((total, rows, owned, channels), bf16),
+            pltpu.VMEM((total // 2, rows, owned, channels), bf16),
             dma((groups,)),
             dma((4,)),
             dma((2, groups)),

time: 44.1 us -> 43.9 us (level)
  no operation moved by 1% of the time
where the time goes in v5:
time: 43.9 us; the launch traced here: 43.8 us
  Pallas kernels  43.1 us (98%)
  local copies, waits for them, and re-layouts  0.71 us (2%)
    pallas_call x1, Pallas kernels, body(): pl.pallas_call(functools.partial(kernel, tiles), out_shape=pltpu.VMEM((to...  43.1 us

profile of v5, /device:TPU:30, one launch (start us, length us, event | category | flops | bytes accessed | tf_op | source)
XLA Modules:
  0.0 43.8 jit_solution(14034896808827313339)
XLA Ops:
  0.0 43.1 %shard_map.55 = bf16[4,2,64,256]{3,2,1,0:T(8,128)(2,1)S(1)} custom-call(bf16[8,2,64,256]{3,2,1,0:T(8,128)(2,1)} %frames.1, bf16[1,2,2304,256]{3,2,1,0:T(8,128)(2,1)} %sw_hbm.1, bf16[1,2,768,256]{3,2,1,0:T(8,128)(2,1)} %tw_hbm.1, s32[1,96]{1,0:T(1,128)} %ramp.1, s32[1,2]{1,0:T(1,128)} %inter.1), custom_call_target="tpu_custom_call" | custom-call | tf_op jit(solution)/shard_map/pallas_call | solution.py:296
  43.1 0.7 %copy.7 = bf16[4,2,64,256]{3,2,1,0:T(8,128)(2,1)} copy(bf16[4,2,64,256]{3,2,1,0:T(8,128)(2,1)S(1)} %shard_map.55) | data formatting | bytes 524288
